TPU v7x, 1024 devices: a whole 4x8x16 slice. The times are simulated.
1024 devices in a mesh: kv: 8 (over y), key: 16 (over z), tok: 8 (over x, core).
Axes of the slice: x: 4, y: 8, z: 16, core: 2. Of those that a mesh axis runs over, the one named last changes fastest.
Arguments:
- queries: bfloat16 [4096, 8192], P('key', ('kv', 'tok')), may hold values from -200 to 200
- keys: bfloat16 [4096, 1024], P('key', 'kv'), may hold values from -8 to 8
- values: bfloat16 [4096, 1024], P('key', 'kv'), may hold values from -6 to 6
- doc_ids: int32 [4096], replicated, may hold values from 0 to 5, never falling along the last dimension, each value on 1 to 2048 neighbouring positions
- out_weight: bfloat16 [8192, 8192], P('kv', 'tok'), may hold values from -0.0625 to 0.0625
Outputs:
- mixed: bfloat16 [4096, 8192], P(('key', 'kv'), 'tok')
Inputs may be any that keep to these rules, and one draw needn't show every extreme that they name: `doc_ids`: document numbers never fall along the window; a document covers at most 2048 positions and some document covers exactly that many.
All inputs are finite; a program needn't handle non-finite values.
Results may differ from a plain program's by a relative error of at most 0.014.
Values may be sent and summed in bfloat16 or wider, within the bound.
No kernel may reach another device: no remote copies, remote signals or barrier semaphores. Data moves between devices by JAX's collectives and lax.ppermute only.
A program may use at most 32 MiB of HBM per device.

v0:
```python
import math

import jax
import jax.numpy as jnp
from jax import lax
from jax.experimental import pallas as pl
from jax.experimental.pallas import tpu as pltpu
from jax.sharding import PartitionSpec as P


HEAD_SIZE = 128
REACH = 8
LOW = -1e30
MOST_DOC = 5
LANES = 128
CORES = 2
PAIR = 2
FACTOR = math.log2(math.e) / math.sqrt(HEAD_SIZE)

VMEM = pl.BlockSpec(memory_space=pltpu.VMEM)


def dot(a, b, contract):
    return lax.dot_general(a, b, (contract, ((), ())), preferred_element_type=jnp.float32)


def start_kernel(keys_ref, values_ref, out_ref, sems):
    rows = out_ref.shape[0]
    tok = lax.axis_index("tok")
    shift = shift_of(tok // CORES, lax.rem(tok, CORES))
    begin = pl.multiple_of(lax.rem(tok, CORES) * rows, rows)

    @pl.when(lax.axis_index("key") + shift < lax.axis_size("key"))
    def _():
        copies = [
            pltpu.make_async_copy(
                source.at[pl.ds(begin, rows), :],
                out_ref.at[:, pl.ds(place * HEAD_SIZE, HEAD_SIZE)],
                sems.at[place],
            )
            for place, source in enumerate((keys_ref, values_ref))
        ]
        for copy in copies:
            copy.start()
        for copy in copies:
            copy.wait()


def start(keys, values):
    hbm = pl.BlockSpec(memory_space=pltpu.HBM)
    return pl.pallas_call(
        start_kernel,
        out_shape=jax.ShapeDtypeStruct((keys.shape[0] // CORES, 2 * HEAD_SIZE), jnp.bfloat16),
        in_specs=[hbm] * 2,
        out_specs=VMEM,
        scratch_shapes=[pltpu.SemaphoreType.DMA((2,))],
        compiler_params=pltpu.CompilerParams(vmem_limit_bytes=4 << 20),
        name="start",
    )(*(pltpu.with_memory_space_constraint(x, pltpu.HBM) for x in (keys, values)))


def load_kernel(queries_ref, keys_ref, values_ref, docs_ref, own_ref, docs_out_ref, sems):
    copies = [
        pltpu.make_async_copy(source, own_ref.at[place], sems.at[place])
        for place, source in enumerate((keys_ref, values_ref, queries_ref))
    ]
    copies.append(pltpu.make_async_copy(docs_ref, docs_out_ref, sems.at[3]))
    for copy in copies:
        copy.start()
    for copy in copies:
        copy.wait()


def load(*arrays):
    _, keys, _, docs = arrays
    hbm = pl.BlockSpec(memory_space=pltpu.HBM)
    return pl.pallas_call(
        load_kernel,
        out_shape=[
            jax.ShapeDtypeStruct((3,) + keys.shape, jnp.bfloat16),
            jax.ShapeDtypeStruct(docs.shape, jnp.int32),
        ],
        in_specs=[hbm] * 4,
        out_specs=[VMEM] * 2,
        scratch_shapes=[pltpu.SemaphoreType.DMA((4,))],
        compiler_params=pltpu.CompilerParams(vmem_limit_bytes=4 << 20),
        name="load",
    )(*(pltpu.with_memory_space_constraint(x, pltpu.HBM) for x in arrays))


def find_first(docs_ref, own, query_count):
    docs = docs_ref[...]
    place = lax.broadcasted_iota(jnp.int32, (1, query_count), 1)
    place = (place + own * query_count).astype(jnp.float32)
    first = jnp.zeros((1, query_count), jnp.float32)
    for number in range(1, MOST_DOC + 1):
        smaller = jnp.where(docs < number, 1.0, 0.0)
        begins = jnp.sum(jnp.sum(smaller, axis=0, keepdims=True), axis=1, keepdims=True)
        first = jnp.where(begins <= place, jnp.maximum(first, begins), first)
    return first


def shift_of(chip, core):
    return jnp.where(core == 0, REACH - PAIR * chip, PAIR + PAIR * chip)


def pick_kernel(own_ref, held_ref, out_ref):
    own, tok = lax.axis_index("key"), lax.axis_index("tok")
    rows = held_ref.shape[0]
    takers = out_ref.shape[0] // PAIR
    swapped = (lax.rem(own, PAIR) == 0) & (shift_of(tok // CORES, lax.rem(tok, CORES)) == REACH)
    held = held_ref[...]
    for taker in range(takers):
        out_ref[taker] = held

    @pl.when(swapped)
    def _():
        begin = pl.multiple_of(lax.rem(tok, CORES) * rows, rows)
        half = pl.ds(begin, rows)
        pair = jnp.concatenate([own_ref[0, half, :], own_ref[1, half, :]], axis=1)
        for taker in range(takers):
            out_ref[takers + taker] = pair

    @pl.when(jnp.logical_not(swapped))
    def _():
        for taker in range(takers):
            out_ref[takers + taker] = held_ref[...]


def pick(own, held, taker_count):
    return pl.pallas_call(
        pick_kernel,
        out_shape=jax.ShapeDtypeStruct((taker_count,) + held.shape, jnp.bfloat16),
        in_specs=[VMEM, VMEM],
        out_specs=VMEM,
        compiler_params=pltpu.CompilerParams(vmem_limit_bytes=8 << 20),
        name="pick",
    )(own, held)


def mask_half(scores, own, core, first, blocks_shape, query_count):
    source_count, rows, _ = blocks_shape
    row = lax.broadcasted_iota(jnp.int32, (rows, query_count), 0).astype(jnp.float32)
    chips = source_count // PAIR
    pieces = []
    for source in range(source_count):
        parity, chip = source // chips, source % chips
        shift = shift_of(chip, core)
        if parity == 0:
            shift = jnp.where((lax.rem(own, PAIR) == 1) & (shift == REACH), 0, shift)
        number = own // PAIR * PAIR + parity - shift
        start = number * query_count + core * rows
        allowed = row >= first - start.astype(jnp.float32)
        pieces.append(jnp.where(allowed, scores[source * rows : (source + 1) * rows] * FACTOR, LOW))
    return pieces


def near_kernel(docs_ref, own_ref, blocks_ref, first_ref, stats_ref, sums_ref):
    own, core = lax.axis_index("key"), lax.rem(lax.axis_index("tok"), CORES)
    query_count = first_ref.shape[1]
    first = find_first(docs_ref, own, query_count)
    first_ref[...] = first
    blocks = blocks_ref[...].reshape(-1, 2 * HEAD_SIZE)
    queries = own_ref[2]
    scores = dot(blocks[:, :HEAD_SIZE], queries, ((1,), (1,)))
    pieces = mask_half(scores, own, core, first, blocks_ref.shape, query_count)
    scores = dot(own_ref[0], queries, ((1,), (1,)))
    row = lax.broadcasted_iota(jnp.int32, scores.shape, 0)
    lane = lax.broadcasted_iota(jnp.int32, scores.shape, 1)
    begin = first - (own * query_count).astype(jnp.float32)
    allowed = (row <= lane) & (row.astype(jnp.float32) >= begin)
    pieces.append(jnp.where(allowed, scores * FACTOR, LOW))
    scores = jnp.concatenate(pieces, axis=0)
    highest = jnp.max(scores, axis=0, keepdims=True)
    weights = jnp.exp2(scores - highest)
    stats_ref[0:1, :] = highest
    stats_ref[1:2, :] = jnp.sum(weights, axis=0, keepdims=True)
    values = jnp.concatenate([blocks[:, HEAD_SIZE:], own_ref[1]], axis=0)
    sums_ref[...] = dot(values, weights.astype(jnp.bfloat16), ((0,), (0,)))


def far_kernel(first_ref, own_ref, blocks_ref, stats_ref, sums_ref, out_ref):
    own, core = lax.axis_index("key"), lax.rem(lax.axis_index("tok"), CORES)
    query_count = first_ref.shape[1]
    blocks = blocks_ref[...].reshape(-1, 2 * HEAD_SIZE)
    scores = dot(blocks[:, :HEAD_SIZE], own_ref[2], ((1,), (1,)))
    pieces = mask_half(scores, own, 1 - core, first_ref[...], blocks_ref.shape, query_count)
    scores = jnp.concatenate(pieces, axis=0)
    before = stats_ref[0:1, :]
    highest = jnp.maximum(before, jnp.max(scores, axis=0, keepdims=True))
    weights = jnp.exp2(scores - highest)
    keep = jnp.exp2(before - highest)
    total = keep * stats_ref[1:2, :] + jnp.sum(weights, axis=0, keepdims=True)
    weighted = dot(blocks[:, HEAD_SIZE:], weights.astype(jnp.bfloat16), ((0,), (0,)))
    attn = ((keep * sums_ref[...] + weighted) * (1.0 / total)).astype(jnp.bfloat16)
    for target in range(out_ref.shape[0]):
        out_ref[target] = attn


def cost(query_count, key_count):
    scores = query_count * key_count
    return pl.CostEstimate(
        flops=4 * HEAD_SIZE * scores, transcendentals=scores, bytes_accessed=1 << 20
    )


def attend_near(docs, own, blocks):
    query_count = own.shape[1]
    return pl.pallas_call(
        near_kernel,
        out_shape=[
            jax.ShapeDtypeStruct((1, query_count), jnp.float32),
            jax.ShapeDtypeStruct((8, query_count), jnp.float32),
            jax.ShapeDtypeStruct((HEAD_SIZE, query_count), jnp.float32),
        ],
        in_specs=[VMEM] * 3,
        out_specs=[VMEM] * 3,
        compiler_params=pltpu.CompilerParams(vmem_limit_bytes=12 << 20),
        cost_estimate=cost(query_count, blocks.shape[0] * blocks.shape[1] + query_count),
        name="near",
    )(docs, own, blocks)


def attend_far(first, own, blocks, stats, sums, target_count):
    query_count = first.shape[1]
    return pl.pallas_call(
        far_kernel,
        out_shape=jax.ShapeDtypeStruct((target_count, HEAD_SIZE, query_count), jnp.bfloat16),
        in_specs=[VMEM] * 5,
        out_specs=VMEM,
        compiler_params=pltpu.CompilerParams(vmem_limit_bytes=12 << 20),
        cost_estimate=cost(query_count, blocks.shape[0] * blocks.shape[1]),
        name="far",
    )(first, own, blocks, stats, sums)


def exchange(x, axis, groups=None):
    return lax.all_to_all(x, axis, 0, 0, tiled=True, axis_index_groups=groups)


def per_device(queries, keys, values, doc_ids, out_weight):
    key_count, tok_count, kv_count = (lax.axis_size(name) for name in ("key", "tok", "kv"))
    row_count = queries.shape[0]
    chips = tok_count // CORES
    beside = [
        [(begin + parity) * tok_count + chip * CORES + core for parity in range(PAIR) for chip in range(chips)]
        for begin in range(0, key_count, PAIR)
        for core in range(CORES)
    ]
    shifts = [REACH - tok if tok % CORES == 0 else PAIR + tok - 1 for tok in range(tok_count)]
    later = [
        (begin * tok_count + tok, (begin + shifts[tok]) * tok_count + tok)
        for begin in range(key_count)
        for tok in range(tok_count)
        if begin + shifts[tok] < key_count
    ]
    half = start(keys, values)
    held = lax.ppermute(half, ("key", "tok"), later)
    own, docs = load(queries, keys, values, doc_ids.reshape(-1, LANES))
    blocks = exchange(pick(own, held, PAIR * chips), ("key", "tok"), beside)
    other_blocks = lax.ppermute(blocks, "tok", [(i, i ^ 1) for i in range(tok_count)])
    first, stats, sums = attend_near(docs, own, blocks)
    attn = attend_far(first, own, other_blocks, stats, sums, tok_count)
    attn = exchange(attn, "tok").reshape(tok_count * HEAD_SIZE, row_count)
    total = jnp.einsum("kq,kn->qn", attn, out_weight, preferred_element_type=jnp.float32)
    total = total.astype(jnp.bfloat16).reshape(kv_count, row_count // kv_count, -1)
    shares = exchange(total, "kv")
    return jnp.sum(shares.astype(jnp.float32), axis=0).astype(jnp.bfloat16)


def solution(mesh):
    placed = (P("key", ("kv", "tok")), P("key", "kv"), P("key", "kv"), P(), P("kv", "tok"))

    return jax.shard_map(
        per_device, mesh=mesh, in_specs=placed, out_specs=P(("key", "kv"), "tok"), check_vma=False
    )
```

profile of v0, /device:TPU:2, one launch (start us, length us, event | category | flops | bytes accessed | tf_op | source)
XLA Modules:
  0.0 76.9 jit_solution(672419826024859210)
XLA Ops:
  0.0 0.0 copy-start
  0.0 0.9 %start.1 = bf16[128,256]{1,0:T(8,128)(2,1)S(1)} custom-call(bf16[256,128]{1,0:T(8,128)(2,1)} %keys_ref.3, bf16[256,128]{1,0:T(8,128)(2,1)} %values_ref.3), custom_call_target="tpu_custom_call" | custom-call | tf_op jit(solution)/shard_map/start/pallas_call | solution.py:51
  1.0 14.5 %collective-permute-start = (bf16[128,256]{1,0:T(8,128)(2,1)S(1)}, bf16[128,256]{1,0:T(8,128)(2,1)S(1)}, u32[]{:S(2)}, u32[]{:S(2)}) collective-permute-start(bf16[128,256]{1,0:T(8,128)(2,1)S(1)} %start.1), channel_id=1, source_target_pairs={{0,64},{1,17},{2,50},{3,35},{4,36},{5,53},{6,22},{7,71},{8,72},{9,... | collective-permute-start | bytes 196616 | tf_op jit(solution)/shard_map/ppermute | solution.py:258
  15.5 0.9 %load.1 = (bf16[3,256,128]{2,1,0:T(8,128)(2,1)S(1)}, s32[32,128]{1,0:T(8,128)S(1)}) custom-call(bf16[256,128]{1,0:T(8,128)(2,1)} %queries_ref.1, bf16[256,128]{1,0:T(8,128)(2,1)} %keys_ref.3, bf16[256,128]{1,0:T(8,128)(2,1)} %values_ref.3, s32[32,128]{1,0:T(8,128)} %bitcast.7), custom_call_target="tpu_custom_call" | custom-call | tf_op jit(solution)/shard_map/load/pallas_call | solution.py:77
  16.4 0.9 %collective-permute-done.held_ref = bf16[128,256]{1,0:T(8,128)(2,1)S(1)} collective-permute-done((bf16[128,256]{1,0:T(8,128)(2,1)S(1)}, bf16[128,256]{1,0:T(8,128)(2,1)S(1)}, u32[]{:S(2)}, u32[]{:S(2)}) %collective-permute-start) | collective-permute-done | bytes 65568 | tf_op jit(solution)/shard_map/ppermute | solution.py:258
  17.4 16.5 %all_to_all.15.blocks_ref = bf16[8,128,256]{2,1,0:T(8,128)(2,1)S(1)} all-to-all(bf16[8,128,256]{2,1,0:T(8,128)(2,1)S(1)} %pick.1), channel_id=1, replica_groups={{0,2,4,6,8,10,12,14},{1,3,5,7,9,11,13,15},{16,18,20,22,24,26,28,30},{17..., dimensions={0} | all-to-all | bytes 1048576 | tf_op jit(solution)/shard_map/all_to_all | solution.py:238
  33.9 1.9 %collective-permute-start.1 = (bf16[8,128,256]{2,1,0:T(8,128)(2,1)S(1)}, bf16[8,128,256]{2,1,0:T(8,128)(2,1)S(1)}, u32[]{:S(2)}, u32[]{:S(2)}) collective-permute-start(bf16[8,128,256]{2,1,0:T(8,128)(2,1)S(1)} %all_to_all.15.blocks_ref), channel_id=1, source_target_pairs={{0,1},{1,0},{2,3},{3,2},{4,5},{5,4},{6,7},{7,6},{8,9},{9,8},{10,11... | collective-permute-start | bytes 1572872 | tf_op jit(solution)/shard_map/ppermute | solution.py:261
  35.8 0.9 %near.1 = (f32[1,256]{1,0:T(1,128)S(1)}, f32[8,256]{1,0:T(8,128)S(1)}, f32[128,256]{1,0:T(8,128)S(1)}) custom-call(s32[32,128]{1,0:T(8,128)S(1)} %get-tuple-element.10.docs_ref, bf16[3,256,128]{2,1,0:T(8,128)(2,1)S(1)} %get-tuple-element.11.own_ref, bf16[8,128,256]{2,1,0:T(8,128)(2,1)S(1)} %all_to_all.15.blocks_ref), custom_call_target="tpu_custom_call" | custom-call | flops 167772160 | bytes 1048576 | tf_op jit(solution)/shard_map/near/pallas_call | solution.py:209
  36.7 1.0 %collective-permute-done.1.blocks_ref = bf16[8,128,256]{2,1,0:T(8,128)(2,1)S(1)} collective-permute-done((bf16[8,128,256]{2,1,0:T(8,128)(2,1)S(1)}, bf16[8,128,256]{2,1,0:T(8,128)(2,1)S(1)}, u32[]{:S(2)}, u32[]{:S(2)}) %collective-permute-start.1) | collective-permute-done | bytes 524320 | tf_op jit(solution)/shard_map/ppermute | solution.py:261
  37.7 0.7 far.1
  38.4 13.0 %all_to_all.16 = bf16[8,128,256]{2,1,0:T(8,128)(2,1)S(1)} all-to-all(bf16[8,128,256]{2,1,0:T(8,128)(2,1)S(1)} %far.1), channel_id=1, replica_groups=mesh['kv'=8,'key'=16,'tok'=8] {'tok'}, dimensions={0} | all-to-all | bytes 1048576 | tf_op jit(solution)/shard_map/all_to_all | solution.py:238
  51.4 0.0 copy-done
  51.4 0.7 convolution_convert_fusion
  52.2 24.0 %all_to_all.17 = bf16[8,32,1024]{2,1,0:T(8,128)(2,1)S(1)} all-to-all(bf16[8,32,1024]{2,1,0:T(8,128)(2,1)S(1)} %bitcast.6), channel_id=1, replica_groups=mesh['kv'=8,'key'=16,'tok'=8] {'kv'}, dimensions={0} | all-to-all | bytes 1048576 | tf_op jit(solution)/shard_map/all_to_all | solution.py:238
  76.2 0.7 reduce_sum.12
  (1 shorter events, 0.0 us)
Async XLA Ops:
  0.0 51.4 %copy-start = (bf16[1024,1024]{1,0:T(8,128)(2,1)S(1)}, bf16[1024,1024]{1,0:T(8,128)(2,1)}, u32[]{:S(2)}) copy-start(bf16[1024,1024]{1,0:T(8,128)(2,1)} %param.9) | copy-start | bytes 6291460
  1.0 16.4 %collective-permute-start = (bf16[128,256]{1,0:T(8,128)(2,1)S(1)}, bf16[128,256]{1,0:T(8,128)(2,1)S(1)}, u32[]{:S(2)}, u32[]{:S(2)}) collective-permute-start(bf16[128,256]{1,0:T(8,128)(2,1)S(1)} %start.1), channel_id=1, source_target_pairs={{0,64},{1,17},{2,50},{3,35},{4,36},{5,53},{6,22},{7,71},{8,72},{9,... | collective-permute-start | bytes 196616 | tf_op jit(solution)/shard_map/ppermute | solution.py:258
  33.9 3.8 %collective-permute-start.1 = (bf16[8,128,256]{2,1,0:T(8,128)(2,1)S(1)}, bf16[8,128,256]{2,1,0:T(8,128)(2,1)S(1)}, u32[]{:S(2)}, u32[]{:S(2)}) collective-permute-start(bf16[8,128,256]{2,1,0:T(8,128)(2,1)S(1)} %all_to_all.15.blocks_ref), channel_id=1, source_target_pairs={{0,1},{1,0},{2,3},{3,2},{4,5},{5,4},{6,7},{7,6},{8,9},{9,8},{10,11... | collective-permute-start | bytes 1572872 | tf_op jit(solution)/shard_map/ppermute | solution.py:261
where the time goes:
time: 77.2 us; the launch traced here: 76.9 us
  blocking collectives  53.5 us (69%)
  starting transfers between devices  16.5 us (21%)
  Pallas kernels  3.53 us (5%)
  waiting for transfers between devices  1.89 us (2%)
    all_to_all x3, blocking collectives, exchange(): return lax.all_to_all(x, axis, 0, 0, tiled=True, axis_index_groups=groups)  53.5 us
    ppermute x1, starting transfers between devices, per_device(): held = lax.ppermute(half, ('key', 'tok'), later)  14.5 us
    ppermute x1, starting transfers between devices, per_device(): lax.ppermute(blocks, 'tok', [(i, i ^ 1) for i in range(tok_count)])  1.94 us
  transfers between devices with their start and end apart: 2, of which 2 were waited for; matrix products, arithmetic and copies ran while one was open for 0% of the time, Pallas kernels for 2%

commit v1 on v0

--- a/solution.py
+++ b/solution.py
@@ -232,6 +232,24 @@
         cost_estimate=cost(query_count, blocks.shape[0] * blocks.shape[1]),
         name="far",
     )(first, own, blocks, stats, sums)
+
+
+def sum_kernel(shares_ref, out_ref):
+    total = shares_ref[0].astype(jnp.float32)
+    for place in range(1, shares_ref.shape[0]):
+        total += shares_ref[place].astype(jnp.float32)
+    out_ref[...] = total.astype(jnp.bfloat16)
+
+
+def sum_shares(shares):
+    return pl.pallas_call(
+        sum_kernel,
+        out_shape=jax.ShapeDtypeStruct(shares.shape[1:], jnp.bfloat16),
+        in_specs=[VMEM],
+        out_specs=VMEM,
+        compiler_params=pltpu.CompilerParams(vmem_limit_bytes=4 << 20),
+        name="sum_shares",
+    )(shares)
 
 
 def exchange(x, axis, groups=None):
@@ -264,8 +282,7 @@
     attn = exchange(attn, "tok").reshape(tok_count * HEAD_SIZE, row_count)
     total = jnp.einsum("kq,kn->qn", attn, out_weight, preferred_element_type=jnp.float32)
     total = total.astype(jnp.bfloat16).reshape(kv_count, row_count // kv_count, -1)
-    shares = exchange(total, "kv")
-    return jnp.sum(shares.astype(jnp.float32), axis=0).astype(jnp.bfloat16)
+    return sum_shares(exchange(total, "kv"))
 
 
 def solution(mesh):

time: 77.2 us -> 77.2 us (level)
  no operation moved by 1% of the time
where the time goes in v1:
time: 77.2 us; the launch traced here: 76.9 us
  blocking collectives  53.5 us (69%)
  starting transfers between devices  16.5 us (21%)
  Pallas kernels  4.23 us (5%)
  waiting for transfers between devices  1.89 us (2%)
    all_to_all x3, blocking collectives, exchange(): return lax.all_to_all(x, axis, 0, 0, tiled=True, axis_index_groups=groups)  53.5 us
    ppermute x1, starting transfers between devices, per_device(): held = lax.ppermute(half, ('key', 'tok'), later)  14.5 us
    ppermute x1, starting transfers between devices, per_device(): lax.ppermute(blocks, 'tok', [(i, i ^ 1) for i in range(tok_count)])  1.94 us
  transfers between devices with their start and end apart: 2, of which 2 were waited for; matrix products, arithmetic and copies ran while one was open for 0% of the time, Pallas kernels for 2%

profile of v1, /device:TPU:2, one launch (start us, length us, event | category | flops | bytes accessed | tf_op | source)
XLA Modules:
  0.0 76.9 jit_solution(8054047119493939192)
XLA Ops:
  0.0 0.0 copy-start
  0.0 0.9 %start.1 = bf16[128,256]{1,0:T(8,128)(2,1)S(1)} custom-call(bf16[256,128]{1,0:T(8,128)(2,1)} %keys_ref.3, bf16[256,128]{1,0:T(8,128)(2,1)} %values_ref.3), custom_call_target="tpu_custom_call" | custom-call | tf_op jit(solution)/shard_map/start/pallas_call | solution.py:51
  1.0 14.5 %collective-permute-start = (bf16[128,256]{1,0:T(8,128)(2,1)S(1)}, bf16[128,256]{1,0:T(8,128)(2,1)S(1)}, u32[]{:S(2)}, u32[]{:S(2)}) collective-permute-start(bf16[128,256]{1,0:T(8,128)(2,1)S(1)} %start.1), channel_id=1, source_target_pairs={{0,64},{1,17},{2,50},{3,35},{4,36},{5,53},{6,22},{7,71},{8,72},{9,... | collective-permute-start | bytes 196616 | tf_op jit(solution)/shard_map/ppermute | solution.py:276
  15.5 0.9 %load.1 = (bf16[3,256,128]{2,1,0:T(8,128)(2,1)S(1)}, s32[32,128]{1,0:T(8,128)S(1)}) custom-call(bf16[256,128]{1,0:T(8,128)(2,1)} %queries_ref.1, bf16[256,128]{1,0:T(8,128)(2,1)} %keys_ref.3, bf16[256,128]{1,0:T(8,128)(2,1)} %values_ref.3, s32[32,128]{1,0:T(8,128)} %bitcast.7), custom_call_target="tpu_custom_call" | custom-call | tf_op jit(solution)/shard_map/load/pallas_call | solution.py:77
  16.4 0.9 %collective-permute-done.held_ref = bf16[128,256]{1,0:T(8,128)(2,1)S(1)} collective-permute-done((bf16[128,256]{1,0:T(8,128)(2,1)S(1)}, bf16[128,256]{1,0:T(8,128)(2,1)S(1)}, u32[]{:S(2)}, u32[]{:S(2)}) %collective-permute-start) | collective-permute-done | bytes 65568 | tf_op jit(solution)/shard_map/ppermute | solution.py:276
  17.4 16.5 %all_to_all.15.blocks_ref = bf16[8,128,256]{2,1,0:T(8,128)(2,1)S(1)} all-to-all(bf16[8,128,256]{2,1,0:T(8,128)(2,1)S(1)} %pick.1), channel_id=1, replica_groups={{0,2,4,6,8,10,12,14},{1,3,5,7,9,11,13,15},{16,18,20,22,24,26,28,30},{17..., dimensions={0} | all-to-all | bytes 1048576 | tf_op jit(solution)/shard_map/all_to_all | solution.py:256
  33.9 1.9 %collective-permute-start.1 = (bf16[8,128,256]{2,1,0:T(8,128)(2,1)S(1)}, bf16[8,128,256]{2,1,0:T(8,128)(2,1)S(1)}, u32[]{:S(2)}, u32[]{:S(2)}) collective-permute-start(bf16[8,128,256]{2,1,0:T(8,128)(2,1)S(1)} %all_to_all.15.blocks_ref), channel_id=1, source_target_pairs={{0,1},{1,0},{2,3},{3,2},{4,5},{5,4},{6,7},{7,6},{8,9},{9,8},{10,11... | collective-permute-start | bytes 1572872 | tf_op jit(solution)/shard_map/ppermute | solution.py:279
  35.8 0.9 %near.1 = (f32[1,256]{1,0:T(1,128)S(1)}, f32[8,256]{1,0:T(8,128)S(1)}, f32[128,256]{1,0:T(8,128)S(1)}) custom-call(s32[32,128]{1,0:T(8,128)S(1)} %get-tuple-element.10.docs_ref, bf16[3,256,128]{2,1,0:T(8,128)(2,1)S(1)} %get-tuple-element.11.own_ref, bf16[8,128,256]{2,1,0:T(8,128)(2,1)S(1)} %all_to_all.15.blocks_ref), custom_call_target="tpu_custom_call" | custom-call | flops 167772160 | bytes 1048576 | tf_op jit(solution)/shard_map/near/pallas_call | solution.py:209
  36.7 1.0 %collective-permute-done.1.blocks_ref = bf16[8,128,256]{2,1,0:T(8,128)(2,1)S(1)} collective-permute-done((bf16[8,128,256]{2,1,0:T(8,128)(2,1)S(1)}, bf16[8,128,256]{2,1,0:T(8,128)(2,1)S(1)}, u32[]{:S(2)}, u32[]{:S(2)}) %collective-permute-start.1) | collective-permute-done | bytes 524320 | tf_op jit(solution)/shard_map/ppermute | solution.py:279
  37.7 0.7 far.1
  38.4 13.0 %all_to_all.16 = bf16[8,128,256]{2,1,0:T(8,128)(2,1)S(1)} all-to-all(bf16[8,128,256]{2,1,0:T(8,128)(2,1)S(1)} %far.1), channel_id=1, replica_groups=mesh['kv'=8,'key'=16,'tok'=8] {'tok'}, dimensions={0} | all-to-all | bytes 1048576 | tf_op jit(solution)/shard_map/all_to_all | solution.py:256
  51.4 0.0 copy-done
  51.4 0.7 convolution_convert_fusion
  52.2 24.0 %all_to_all.17.shares_ref = bf16[8,32,1024]{2,1,0:T(8,128)(2,1)S(1)} all-to-all(bf16[8,32,1024]{2,1,0:T(8,128)(2,1)S(1)} %bitcast.6), channel_id=1, replica_groups=mesh['kv'=8,'key'=16,'tok'=8] {'kv'}, dimensions={0} | all-to-all | bytes 1048576 | tf_op jit(solution)/shard_map/all_to_all | solution.py:256
  76.2 0.7 sum_shares.1
  (1 shorter events, 0.0 us)
Async XLA Ops:
  0.0 51.4 %copy-start = (bf16[1024,1024]{1,0:T(8,128)(2,1)S(1)}, bf16[1024,1024]{1,0:T(8,128)(2,1)}, u32[]{:S(2)}) copy-start(bf16[1024,1024]{1,0:T(8,128)(2,1)} %param.9) | copy-start | bytes 6291460
  1.0 16.4 %collective-permute-start = (bf16[128,256]{1,0:T(8,128)(2,1)S(1)}, bf16[128,256]{1,0:T(8,128)(2,1)S(1)}, u32[]{:S(2)}, u32[]{:S(2)}) collective-permute-start(bf16[128,256]{1,0:T(8,128)(2,1)S(1)} %start.1), channel_id=1, source_target_pairs={{0,64},{1,17},{2,50},{3,35},{4,36},{5,53},{6,22},{7,71},{8,72},{9,... | collective-permute-start | bytes 196616 | tf_op jit(solution)/shard_map/ppermute | solution.py:276
  33.9 3.8 %collective-permute-start.1 = (bf16[8,128,256]{2,1,0:T(8,128)(2,1)S(1)}, bf16[8,128,256]{2,1,0:T(8,128)(2,1)S(1)}, u32[]{:S(2)}, u32[]{:S(2)}) collective-permute-start(bf16[8,128,256]{2,1,0:T(8,128)(2,1)S(1)} %all_to_all.15.blocks_ref), channel_id=1, source_target_pairs={{0,1},{1,0},{2,3},{3,2},{4,5},{5,4},{6,7},{7,6},{8,9},{9,8},{10,11... | collective-permute-start | bytes 1572872 | tf_op jit(solution)/shard_map/ppermute | solution.py:279
